TPU v7x, 32 devices: a whole 2x2x4 slice. The times are simulated.
32 devices in a mesh: doc: 8 (over y, x, core), vocab: 4 (over z).
Axes of the slice: x: 2, y: 2, z: 4, core: 2. Of those that a mesh axis runs over, the one named last changes fastest.
Arguments:
- tile_values: bfloat16 [8, 4, 24, 128, 128], P('doc', 'vocab'), may hold values from -6 to 6
- tile_rows: int32 [8, 4, 24], P('doc', 'vocab'), may hold values from 0 to 7, as said below
- tile_columns: int32 [8, 4, 24], P('doc', 'vocab'), may hold values from 0 to 3
- counts: int32 [8, 4], P('doc', 'vocab'), may hold values from 7 to 24, as said below
- sketch: bfloat16 [2048, 512], P('vocab'), may hold values from -6 to 6
- query_tiles: int32 [2048, 4, 4], P('doc', 'vocab'), may hold values from 0 to 3
- query_values: float32 [2048, 4, 4, 128], P('doc', 'vocab'), may hold values from -6 to 6
Outputs:
- term_basis: float32 [4, 512, 512], P('vocab', 'doc')
- projections: float32 [2048, 512], P('doc')
Inputs may be any that keep to these rules, and one draw needn't show every extreme that they name: Each device uses its first counts slots; some device uses all 24 slots in every draw. The (tile_rows, tile_columns) pairs of one device's 24 slots are all different. `query_tiles`: A query may name the same term block more than once; the values then add.
All inputs are finite; a program needn't handle non-finite values.
Results may differ from a plain program's by a relative error of at most 0.0016.
Values may be sent and summed in bfloat16 or wider, within the bound.
No kernel may reach another device: no remote copies, remote signals or barrier semaphores. Data moves between devices by JAX's collectives and lax.ppermute only.
A program may use at most 64 MiB of HBM per device.

v0:
```python
import jax
import jax.numpy as jnp
from jax import lax
from jax.sharding import PartitionSpec as P

ROW_TILES = 8
GROUP_SLOTS = 4
precise = lax.Precision.HIGHEST


def query_matrix(query_tiles, query_values, term_tiles):
    slot_tiles = query_tiles[:, 0, :]
    values = query_values[:, 0]
    onehot = (
        slot_tiles[:, :, None] == jnp.arange(term_tiles, dtype=jnp.int32)[None, None, :]
    ).astype(jnp.float32)
    placed = jnp.einsum("qtc,qti->qci", onehot, values, precision=precise)
    return placed.reshape(placed.shape[0], placed.shape[1] * placed.shape[2])


def body(tile_values, tile_rows, tile_columns, counts, sketch, query_tiles, query_values):
    blocks = tile_values[0, 0]
    row_index = tile_rows[0, 0]
    column_index = tile_columns[0, 0]
    used_slots = counts[0, 0]
    tile_edge = blocks.shape[1]
    local_terms = sketch.shape[0]
    sketch_width = sketch.shape[1]
    term_tiles = local_terms // tile_edge
    rounds = (used_slots + GROUP_SLOTS - 1) // GROUP_SLOTS
    sketch_blocks = sketch.reshape(term_tiles, tile_edge, sketch_width)
    slot_lanes = jnp.arange(GROUP_SLOTS, dtype=jnp.int32)

    def forward(step_index, totals):
        offset = step_index * GROUP_SLOTS
        group_blocks = lax.dynamic_slice_in_dim(blocks, offset, GROUP_SLOTS, 0)
        at_rows = lax.dynamic_slice_in_dim(row_index, offset, GROUP_SLOTS, 0)
        at_columns = lax.dynamic_slice_in_dim(column_index, offset, GROUP_SLOTS, 0)
        active = (offset + slot_lanes < used_slots).astype(jnp.float32)
        product = jnp.einsum(
            "sij,sjk->sik",
            group_blocks,
            sketch_blocks[at_columns],
            preferred_element_type=jnp.float32,
        )
        return totals.at[at_rows].add(product * active[:, None, None])

    start_rows = jnp.zeros((ROW_TILES, tile_edge, sketch_width), jnp.float32)
    partial_rows = lax.fori_loop(0, rounds, forward, start_rows)
    reduced = lax.psum_scatter(
        partial_rows.reshape(ROW_TILES * tile_edge, sketch_width),
        "vocab",
        scatter_dimension=0,
        tiled=True,
    )
    sketched = lax.all_gather(reduced.astype(jnp.bfloat16), "vocab", axis=0, tiled=True)
    sketched_blocks = sketched.reshape(ROW_TILES, tile_edge, sketch_width)

    def backward(step_index, totals):
        offset = step_index * GROUP_SLOTS
        group_blocks = lax.dynamic_slice_in_dim(blocks, offset, GROUP_SLOTS, 0)
        at_rows = lax.dynamic_slice_in_dim(row_index, offset, GROUP_SLOTS, 0)
        at_columns = lax.dynamic_slice_in_dim(column_index, offset, GROUP_SLOTS, 0)
        active = (offset + slot_lanes < used_slots).astype(jnp.float32)
        product = jnp.einsum(
            "sij,sik->sjk",
            group_blocks,
            sketched_blocks[at_rows],
            preferred_element_type=jnp.float32,
        )
        return totals.at[at_columns].add(product * active[:, None, None])

    start_terms = jnp.zeros((term_tiles, tile_edge, sketch_width), jnp.float32)
    term_part = lax.fori_loop(0, rounds, backward, start_terms).reshape(local_terms, sketch_width)
    query_dense = query_matrix(query_tiles, query_values, term_tiles)
    vocab_total = local_terms * lax.axis_size("vocab")
    share_rows = local_terms // lax.axis_size("doc")
    term_block = lax.psum(term_part, "doc")
    gram_part = jnp.dot(term_block.T, term_block, precision=precise)
    gram_whole = lax.psum(gram_part, "vocab")
    factor = jnp.linalg.cholesky(gram_whole / vocab_total)
    full_basis = lax.linalg.triangular_solve(
        factor, term_block, left_side=False, lower=True, transpose_a=True
    )
    basis_rows = lax.dynamic_slice_in_dim(
        full_basis, lax.axis_index("doc") * share_rows, share_rows, 0
    )
    local_projection = jnp.dot(query_dense, full_basis, precision=precise)
    projected = lax.psum(local_projection, "vocab")
    scaling = lax.rsqrt(jnp.mean(projected * projected, axis=1, keepdims=True) + 1e-06)
    return (basis_rows[None], projected * scaling)


def solution(mesh):
    return jax.shard_map(
        body,
        mesh=mesh,
        in_specs=(
            P("doc", "vocab", None, None, None),
            P("doc", "vocab", None),
            P("doc", "vocab", None),
            P("doc", "vocab"),
            P("vocab", None),
            P("doc", "vocab", None),
            P("doc", "vocab", None, None),
        ),
        out_specs=(P("vocab", "doc", None), P("doc", None)),
        check_vma=False,
    )
```

profile of v0, /device:TPU:0, one launch (start us, length us, event | category | flops | bytes accessed | tf_op | source)
XLA Modules:
  0.0 461.3 jit_solution(15977622500385682956)
XLA Ops:
  9.7 28.5 %while.24 = (s32[]{:T(128)}, f32[8,128,512]{2,1,0:T(8,128)}, s32[]{:T(128)}, s32[24]{0:T(128)S(1)}, bf16[24,128,128]{2,1,0:T(8,128)(2,1)S(1)}, /*index=5*/s32[24...) while((s32[]{:T(128)}, f32[8,128,512]{2,1,0:T(8,128)}, ...), condition=%wide.region_2.3_spmd.clone, body=%wide.region_0.2_spmd.clone.sunk | while | flops 67634216 | bytes 5903155 | solution.py:49
  11.3 3.2 scatter_fusion
  16.1 3.1 scatter_fusion
  20.9 3.2 scatter_fusion
  25.7 3.2 scatter_fusion
  30.4 3.1 scatter_fusion
  35.2 3.0 scatter_fusion
  38.3 46.3 %reduce-scatter.2.cloned.1.call-done = f32[256,512]{1,0:T(8,128)} async-done(((f32[1024,512]{1,0:T(8,128)}), f32[256,512]{1,0:T(8,128)}) %reduce-scatter.2.cloned.1.call-update) | async-done | bytes 524304 | tf_op jit(solution)/shard_map/reduce_scatter | solution.py:50
  87.6 26.3 %all-gather.2.cloned.1.call-done = bf16[1024,512]{1,0:T(8,128)(2,1)} async-done(((bf16[256,512]{1,0:T(8,128)(2,1)}), bf16[1024,512]{1,0:T(8,128)(2,1)}) %all-gather.2.cloned.1.call-update) | async-done | bytes 1048592 | tf_op jit(solution)/shard_map/all_gather | solution.py:56
  114.1 29.6 %while.25 = (s32[]{:T(128)}, f32[4,128,512]{2,1,0:T(8,128)S(1)}, s32[]{:T(128)}, s32[24]{0:T(128)S(1)}, bf16[24,128,128]{1,2,0:T(8,128)(2,1)}, /*index=5*/s32[24...) while((s32[]{:T(128)}, f32[4,128,512]{2,1,0:T(8,128)S(1)}, ...), condition=%wide.region_6.7_spmd.clone, body=%wide.region_4.6_spmd.clone.sunk | while | flops 67634216 | bytes 5902659 | solution.py:74
  144.8 56.1 %all-reduce.5.cloned.1.call-done = f32[512,512]{1,0:T(8,128)} async-done(((f32[512,512]{1,0:T(8,128)}), f32[512,512]{1,0:T(8,128)}) %all-reduce.5.cloned.1.call-update) | async-done | bytes 1048592 | tf_op jit(solution)/shard_map/psum | solution.py:78
  201.0 4.4 fusion.45
  207.1 49.6 %all-reduce.7.cloned.1.call-done = f32[512,512]{0,1:T(8,128)} async-done(((f32[512,512]{0,1:T(8,128)}), f32[512,512]{0,1:T(8,128)}) %all-reduce.7.cloned.1.call-update) | async-done | bytes 1048592 | tf_op jit(solution)/shard_map/psum | solution.py:80
  261.9 11.7 %cholesky.104 = f32[128,128]{1,0:T(8,128)S(1)} custom-call(f32[128,128]{1,0:T(8,128)S(1)} %cholesky.266), custom_call_target="Cholesky" | custom-call | tf_op jit(solution)/shard_map/jit(cholesky)/cholesky | solution.py:81
  273.8 9.8 %custom-call.30 = f32[1,128,128]{1,2,0:T(8,128)S(1)} custom-call(f32[1,128,128]{2,1,0:T(8,128)S(1)} %get-tuple-element.217), custom_call_target="InvertDiagBlocksLowerTriangular" | custom-call | tf_op jit(solution)/shard_map/jit(cholesky)/cholesky | solution.py:81
  286.2 11.8 %cholesky.217 = f32[128,128]{1,0:T(8,128)S(1)} custom-call(f32[128,128]{1,0:T(8,128)S(1)} %cholesky.270), custom_call_target="Cholesky" | custom-call | tf_op jit(solution)/shard_map/jit(cholesky)/cholesky | solution.py:81
  298.0 9.8 %custom-call.31 = f32[1,128,128]{1,2,0:T(8,128)S(1)} custom-call(f32[1,128,128]{2,1,0:T(8,128)S(1)} %get-tuple-element.214), custom_call_target="InvertDiagBlocksLowerTriangular" | custom-call | tf_op jit(solution)/shard_map/jit(cholesky)/cholesky | solution.py:81
  309.4 11.7 %cholesky.238 = f32[128,128]{1,0:T(8,128)S(1)} custom-call(f32[128,128]{1,0:T(8,128)S(1)} %cholesky.275), custom_call_target="Cholesky" | custom-call | tf_op jit(solution)/shard_map/jit(cholesky)/cholesky | solution.py:81
  321.8 9.8 %custom-call.32 = f32[1,128,128]{1,2,0:T(8,128)S(1)} custom-call(f32[1,128,128]{2,1,0:T(8,128)S(1)} %get-tuple-element.211), custom_call_target="InvertDiagBlocksLowerTriangular" | custom-call | tf_op jit(solution)/shard_map/jit(cholesky)/cholesky | solution.py:81
  333.1 11.9 %cholesky.255 = f32[128,128]{1,0:T(8,128)S(1)} custom-call(f32[128,128]{1,0:T(8,128)S(1)} %convolution_subtract_fusion.5), custom_call_target="Cholesky" | custom-call | tf_op jit(solution)/shard_map/jit(cholesky)/cholesky | solution.py:81
  350.1 13.8 %while.23 = (s32[]{:T(128)}, f32[512,512]{1,0:T(8,128)}, s32[4,2]{0,1:T(2,128)S(1)}, f32[4,128,128]{2,1,0:T(8,128)}, s32[]{:T(128)}) while((s32[]{:T(128)}, f32[512,512]{1,0:T(8,128)}, s32[4,2]{0,1:T(2,128)S(1)}, f32[4,128,128]{2,1,0:T(8,128)}, s32[]{:T(128)}) %tuple.77), condition=%wide.while_cond, body=%wide.while_body.sunk | while | flops 2 | bytes 132705 | solution.py:82
  350.7 2.9 bitcast_dynamic-update-slice_fusion.2
  363.9 40.1 %custom-call.33 = f32[4,128,128]{1,2,0:T(8,128)S(1)} custom-call(f32[4,128,128]{2,1,0:T(8,128)} %get-tuple-element.107), custom_call_target="InvertDiagBlocksLowerTriangular" | custom-call | tf_op jit(solution)/shard_map/triangular_solve | solution.py:82
  414.4 37.1 %all-reduce.9.cloned.1.call-done = f32[256,512]{1,0:T(8,128)} async-done(((f32[256,512]{1,0:T(8,128)}), f32[256,512]{1,0:T(8,128)}) %all-reduce.9.cloned.1.call-update) | async-done | bytes 524304 | tf_op jit(solution)/shard_map/psum | solution.py:89
  (151 shorter events, 85.0 us)
Async XLA Ops:
  7.2 198.9 %copy-start = (f32[256,1,4,128]{3,2,1,0:T(4,128)S(1)}, f32[256,1,4,128]{3,2,1,0:T(4,128)}, u32[]{:S(2)}) copy-start(f32[256,1,4,128]{3,2,1,0:T(4,128)} %param.17) | copy-start | bytes 1572868
  7.2 2.5 copy-start.8
  7.2 2.5 copy-start.7
  7.2 2.5 copy-start.6
  7.2 2.5 copy-start.2
  7.2 77.4 %reduce-scatter.2.cloned.1.call-start = ((), (), s32[]{:S(2)}) async-start(), calls=%async_computation.1 | async-start | bytes 2621440 | tf_op jit(solution)/shard_map/reduce_scatter | solution.py:50
  38.2 75.7 %all-gather.2.cloned.1.call-start = ((), (), s32[]{:S(2)}) async-start(), calls=%async_computation.2 | async-start | bytes 1310720 | tf_op jit(solution)/shard_map/all_gather | solution.py:56
  86.4 114.6 %all-reduce.5.cloned.1.call-start = ((), (), s32[]{:S(2)}) async-start(), calls=%async_computation.3 | async-start | bytes 2097152 | tf_op jit(solution)/shard_map/psum | solution.py:78
  143.7 1.0 copy-start.1
  144.8 61.2 %copy-start.9 = (s32[256,1,4]{0,2,1:T(4,128)S(1)}, s32[256,1,4]{0,2,1:T(4,128)}, u32[]{:S(2)}) copy-start(s32[256,1,4]{0,2,1:T(4,128)} %param.16) | copy-start | bytes 12292
  144.8 111.9 %all-reduce.7.cloned.1.call-start = ((), (), s32[]{:S(2)}) async-start(), calls=%async_computation.4 | async-start | bytes 2097152 | tf_op jit(solution)/shard_map/psum | solution.py:80
  205.4 246.0 %all-reduce.9.cloned.1.call-start = ((), (), s32[]{:S(2)}) async-start(), calls=%async_computation.5 | async-start | bytes 1048576 | tf_op jit(solution)/shard_map/psum | solution.py:89
  256.7 4.0 copy-start.4
  260.9 1.0 copy-start.5
  309.4 94.7 %copy-start.3 = (f32[512,512]{1,0:T(8,128)S(1)}, f32[512,512]{1,0:T(8,128)}, u32[]{:S(2)}) copy-start(f32[512,512]{1,0:T(8,128)} %all-reduce.5.cloned.1.call-done) | copy-start | bytes 3145732
Sparse Core Ops, SparseCore 0:
  38.4 46.1 reduce-scatter.1
  86.7 27.1 all-gather.1
  144.9 56.0 all-reduce.4
  205.5 51.1 all-reduce.6
  413.5 37.9 all-reduce.8
where the time goes:
time: 466 us; the launch traced here: 461 us
  waiting for transfers between devices  215 us (46%)
  other arithmetic  162 us (35%)
  local copies, waits for them, and re-layouts  35.9 us (8%)
  matrix products  28.9 us (6%)
  between operations  17.7 us (4%)
    another operation x14, other arithmetic, body(): factor = jnp.linalg.cholesky(gram_whole / vocab_total)  78.8 us
    psum x1, waiting for transfers between devices, body(): term_block = lax.psum(term_part, 'doc')  56.1 us
    psum x1, waiting for transfers between devices, body(): gram_whole = lax.psum(gram_part, 'vocab')  49.6 us
    reduce_scatter x1, waiting for transfers between devices, body(): lax.psum_scatter(partial_rows.reshape(ROW_TILES * tile_edge, sketch_width...  46.3 us
    another operation x4, other arithmetic, body(): lax.linalg.triangular_solve(factor, term_block, left_side=False, lower=Tr...  41.4 us
    psum x1, waiting for transfers between devices, body(): projected = lax.psum(local_projection, 'vocab')  37.1 us
    all_gather x1, waiting for transfers between devices, body(): lax.all_gather(reduced.astype(jnp.bfloat16), 'vocab', axis=0, tiled=True)  26.3 us
    scatter-add x6, other arithmetic, forward(): return totals.at[at_rows].add(product * active[:, None, None])  18.8 us
  transfers between devices with their start and end apart: 5, of which 5 were waited for; matrix products, arithmetic and copies ran while one was open for 1% of the time, Pallas kernels for 0%

commit v1 on v0

--- a/solution.py
+++ b/solution.py
@@ -53,7 +53,10 @@
         scatter_dimension=0,
         tiled=True,
     )
-    sketched = lax.all_gather(reduced.astype(jnp.bfloat16), "vocab", axis=0, tiled=True)
+    obj = reduced.astype(jnp.bfloat16)
+    sketched = jnp.concatenate(
+        lax.all_to_all(jnp.stack([obj for _ in range(lax.psum(1, "vocab"))], 0), "vocab", 0, 0), 0
+    )
     sketched_blocks = sketched.reshape(ROW_TILES, tile_edge, sketch_width)
 
     def backward(step_index, totals):

time: 466 us -> 469 us (level)
    all_gather x1 -> x0, waiting for transfers between devices: 26.3 us -> none  [body(): lax.all_gather(reduced.astype(jnp.bfloat16), 'vocab', axis=0, tiled=True)]
    all_to_all x0 -> x1, waiting for transfers between devices: none -> 24.4 us  [body(): lax.all_to_all(jnp.stack([obj for _ in range(lax.psum(1, 'vocab'))], 0),...]
    another operation x12 -> x13, local copies, waits for them, and re-layouts: 13.8 us -> 14.9 us
where the time goes in v1:
time: 469 us; the launch traced here: 464 us
  waiting for transfers between devices  213 us (45%)
  other arithmetic  161 us (34%)
  local copies, waits for them, and re-layouts  37 us (8%)
  matrix products  28.9 us (6%)
  between operations  17.7 us (4%)
  starting transfers between devices  4.86 us (1%)
    another operation x14, other arithmetic, body(): factor = jnp.linalg.cholesky(gram_whole / vocab_total)  78.8 us
    psum x1, waiting for transfers between devices, body(): term_block = lax.psum(term_part, 'doc')  55.8 us
    psum x1, waiting for transfers between devices, body(): gram_whole = lax.psum(gram_part, 'vocab')  49.6 us
    reduce_scatter x1, waiting for transfers between devices, body(): lax.psum_scatter(partial_rows.reshape(ROW_TILES * tile_edge, sketch_width...  46.3 us
    another operation x4, other arithmetic, body(): lax.linalg.triangular_solve(factor, term_block, left_side=False, lower=Tr...  41.4 us
    psum x1, waiting for transfers between devices, body(): projected = lax.psum(local_projection, 'vocab')  36.9 us
    all_to_all x1, waiting for transfers between devices, body(): lax.all_to_all(jnp.stack([obj for _ in range(lax.psum(1, 'vocab'))], 0),...  24.4 us
    scatter-add x6, other arithmetic, forward(): return totals.at[at_rows].add(product * active[:, None, None])  18.8 us
  transfers between devices with their start and end apart: 5, of which 5 were waited for; matrix products, arithmetic and copies ran while one was open for 1% of the time, Pallas kernels for 0%

profile of v1, /device:TPU:0, one launch (start us, length us, event | category | flops | bytes accessed | tf_op | source)
XLA Modules:
  0.0 463.6 jit_solution(1966326896568137801)
XLA Ops:
  9.7 28.5 %while.24 = (s32[]{:T(128)}, f32[8,128,512]{2,1,0:T(8,128)}, s32[]{:T(128)}, s32[24]{0:T(128)S(1)}, bf16[24,128,128]{2,1,0:T(8,128)(2,1)S(1)}, /*index=5*/s32[24...) while((s32[]{:T(128)}, f32[8,128,512]{2,1,0:T(8,128)}, ...), condition=%wide.region_2.3_spmd.clone, body=%wide.region_0.2_spmd.clone.sunk | while | flops 67634216 | bytes 5903155 | solution.py:49
  11.3 3.2 scatter_fusion
  16.1 3.1 scatter_fusion
  20.9 3.2 scatter_fusion
  25.7 3.2 scatter_fusion
  30.4 3.1 scatter_fusion
  35.2 3.0 scatter_fusion
  38.2 46.3 %reduce-scatter.2.cloned.1.call-done = f32[256,512]{1,0:T(8,128)} async-done(((f32[1024,512]{1,0:T(8,128)}), f32[256,512]{1,0:T(8,128)}) %reduce-scatter.2.cloned.1.call-update) | async-done | bytes 524304 | tf_op jit(solution)/shard_map/reduce_scatter | solution.py:50
  86.8 4.2 all-to-all-start
  92.3 24.4 %all-to-all-done = bf16[4,256,512]{2,1,0:T(8,128)(2,1)} async-done(((bf16[4,256,512]{2,1,0:T(8,128)(2,1)}), bf16[4,256,512]{2,1,0:T(8,128)(2,1)}, u32[]{:S(2)}, u32[]{:S(2)}) %all-to-all-start) | async-done | bytes 1048608 | tf_op jit(solution)/shard_map/all_to_all | solution.py:58
  116.8 29.6 %while.25 = (s32[]{:T(128)}, f32[4,128,512]{2,1,0:T(8,128)S(1)}, s32[]{:T(128)}, s32[24]{0:T(128)S(1)}, bf16[24,128,128]{1,2,0:T(8,128)(2,1)}, /*index=5*/s32[24...) while((s32[]{:T(128)}, f32[4,128,512]{2,1,0:T(8,128)S(1)}, ...), condition=%wide.region_6.7_spmd.clone, body=%wide.region_4.6_spmd.clone.sunk | while | flops 67634216 | bytes 5902659 | solution.py:77
  147.6 55.8 %all-reduce.5.cloned.1.call-done = f32[512,512]{1,0:T(8,128)} async-done(((f32[512,512]{1,0:T(8,128)}), f32[512,512]{1,0:T(8,128)}) %all-reduce.5.cloned.1.call-update) | async-done | bytes 1048592 | tf_op jit(solution)/shard_map/psum | solution.py:81
  203.4 4.4 fusion.45
  209.5 49.6 %all-reduce.7.cloned.1.call-done = f32[512,512]{0,1:T(8,128)} async-done(((f32[512,512]{0,1:T(8,128)}), f32[512,512]{0,1:T(8,128)}) %all-reduce.7.cloned.1.call-update) | async-done | bytes 1048592 | tf_op jit(solution)/shard_map/psum | solution.py:83
  264.3 11.7 %cholesky.104 = f32[128,128]{1,0:T(8,128)S(1)} custom-call(f32[128,128]{1,0:T(8,128)S(1)} %cholesky.266), custom_call_target="Cholesky" | custom-call | tf_op jit(solution)/shard_map/jit(cholesky)/cholesky | solution.py:84
  276.2 9.8 %custom-call.30 = f32[1,128,128]{1,2,0:T(8,128)S(1)} custom-call(f32[1,128,128]{2,1,0:T(8,128)S(1)} %get-tuple-element.217), custom_call_target="InvertDiagBlocksLowerTriangular" | custom-call | tf_op jit(solution)/shard_map/jit(cholesky)/cholesky | solution.py:84
  288.6 11.8 %cholesky.217 = f32[128,128]{1,0:T(8,128)S(1)} custom-call(f32[128,128]{1,0:T(8,128)S(1)} %cholesky.270), custom_call_target="Cholesky" | custom-call | tf_op jit(solution)/shard_map/jit(cholesky)/cholesky | solution.py:84
  300.4 9.8 %custom-call.31 = f32[1,128,128]{1,2,0:T(8,128)S(1)} custom-call(f32[1,128,128]{2,1,0:T(8,128)S(1)} %get-tuple-element.214), custom_call_target="InvertDiagBlocksLowerTriangular" | custom-call | tf_op jit(solution)/shard_map/jit(cholesky)/cholesky | solution.py:84
  311.8 11.7 %cholesky.238 = f32[128,128]{1,0:T(8,128)S(1)} custom-call(f32[128,128]{1,0:T(8,128)S(1)} %cholesky.275), custom_call_target="Cholesky" | custom-call | tf_op jit(solution)/shard_map/jit(cholesky)/cholesky | solution.py:84
  324.2 9.8 %custom-call.32 = f32[1,128,128]{1,2,0:T(8,128)S(1)} custom-call(f32[1,128,128]{2,1,0:T(8,128)S(1)} %get-tuple-element.211), custom_call_target="InvertDiagBlocksLowerTriangular" | custom-call | tf_op jit(solution)/shard_map/jit(cholesky)/cholesky | solution.py:84
  335.5 11.9 %cholesky.255 = f32[128,128]{1,0:T(8,128)S(1)} custom-call(f32[128,128]{1,0:T(8,128)S(1)} %convolution_subtract_fusion.5), custom_call_target="Cholesky" | custom-call | tf_op jit(solution)/shard_map/jit(cholesky)/cholesky | solution.py:84
  352.5 13.8 %while.23 = (s32[]{:T(128)}, f32[512,512]{1,0:T(8,128)}, s32[4,2]{0,1:T(2,128)S(1)}, f32[4,128,128]{2,1,0:T(8,128)}, s32[]{:T(128)}) while((s32[]{:T(128)}, f32[512,512]{1,0:T(8,128)}, s32[4,2]{0,1:T(2,128)S(1)}, f32[4,128,128]{2,1,0:T(8,128)}, s32[]{:T(128)}) %tuple.77), condition=%wide.while_cond, body=%wide.while_body.sunk | while | flops 2 | bytes 132705 | solution.py:85
  366.3 40.1 %custom-call.33 = f32[4,128,128]{1,2,0:T(8,128)S(1)} custom-call(f32[4,128,128]{2,1,0:T(8,128)} %get-tuple-element.107), custom_call_target="InvertDiagBlocksLowerTriangular" | custom-call | tf_op jit(solution)/shard_map/triangular_solve | solution.py:85
  416.8 36.9 %all-reduce.9.cloned.1.call-done = f32[256,512]{1,0:T(8,128)} async-done(((f32[256,512]{1,0:T(8,128)}), f32[256,512]{1,0:T(8,128)}) %all-reduce.9.cloned.1.call-update) | async-done | bytes 524304 | tf_op jit(solution)/shard_map/psum | solution.py:92
  (151 shorter events, 88.2 us)
Async XLA Ops:
  7.2 201.3 %copy-start = (f32[256,1,4,128]{3,2,1,0:T(4,128)S(1)}, f32[256,1,4,128]{3,2,1,0:T(4,128)}, u32[]{:S(2)}) copy-start(f32[256,1,4,128]{3,2,1,0:T(4,128)} %param.17) | copy-start | bytes 1572868
  7.2 2.5 copy-start.8
  7.2 2.5 copy-start.7
  7.2 2.5 copy-start.6
  7.2 2.5 copy-start.2
  7.2 77.4 %reduce-scatter.2.cloned.1.call-start = ((), (), s32[]{:S(2)}) async-start(), calls=%async_computation.2 | async-start | bytes 2621440 | tf_op jit(solution)/shard_map/reduce_scatter | solution.py:50
  86.8 29.9 %all-to-all-start = ((bf16[4,256,512]{2,1,0:T(8,128)(2,1)}), bf16[4,256,512]{2,1,0:T(8,128)(2,1)}, u32[]{:S(2)}, u32[]{:S(2)}) async-start(bf16[4,256,512]{2,1,0:T(8,128)(2,1)} %stack.2), calls=%async_computation.1 | async-start | bytes 2097152 | tf_op jit(solution)/shard_map/all_to_all | solution.py:58
  91.0 112.4 %all-reduce.5.cloned.1.call-start = ((), (), s32[]{:S(2)}) async-start(), calls=%async_computation.3 | async-start | bytes 2097152 | tf_op jit(solution)/shard_map/psum | solution.py:81
  146.4 1.0 copy-start.1
  147.5 60.8 %copy-start.9 = (s32[256,1,4]{0,2,1:T(4,128)S(1)}, s32[256,1,4]{0,2,1:T(4,128)}, u32[]{:S(2)}) copy-start(s32[256,1,4]{0,2,1:T(4,128)} %param.16) | copy-start | bytes 12292
  147.5 111.6 %all-reduce.7.cloned.1.call-start = ((), (), s32[]{:S(2)}) async-start(), calls=%async_computation.4 | async-start | bytes 2097152 | tf_op jit(solution)/shard_map/psum | solution.py:83
  207.8 245.9 %all-reduce.9.cloned.1.call-start = ((), (), s32[]{:S(2)}) async-start(), calls=%async_computation.5 | async-start | bytes 1048576 | tf_op jit(solution)/shard_map/psum | solution.py:92
  259.1 4.0 copy-start.4
  263.3 1.0 copy-start.5
  311.8 94.6 %copy-start.3 = (f32[512,512]{1,0:T(8,128)S(1)}, f32[512,512]{1,0:T(8,128)}, u32[]{:S(2)}) copy-start(f32[512,512]{1,0:T(8,128)} %all-reduce.5.cloned.1.call-done) | copy-start | bytes 3145732
Sparse Core Ops, SparseCore 0:
  38.4 46.1 reduce-scatter.1
  147.6 55.7 all-reduce.4
  207.9 51.1 all-reduce.6
  415.9 37.7 all-reduce.8
